TPU v7x, 256 devices: a whole 4x4x8 slice. The times are simulated.
256 devices in a mesh: wide: 64 (over z, y, core), narrow: 4 (over x).
Axes of the slice: x: 4, y: 4, z: 8, core: 2. Of those that a mesh axis runs over, the one named last changes fastest.
Arguments:
- hidden_in: bfloat16 [1024, 4096], P('narrow', 'wide'), may hold values from -0.59765625 to 0.59765625
- cached_len: int32 [4], replicated, may hold values from 1 to 4096, 8192 in all
- k_cache: bfloat16 [4, 32768, 128], P('narrow', 'wide'), may hold values from -256 to 256
- v_cache: bfloat16 [4, 32768, 128], P('narrow', 'wide'), may hold values from -24 to 24
- attn_gain: bfloat16 [4096], replicated, may hold values from 0.099609375 to 1.8984375
- ffn_gain: bfloat16 [4096], replicated, may hold values from 0.099609375 to 1.8984375
- wqkv: bfloat16 [6144, 4096], P('wide', 'narrow'), may hold values from -0.09375 to 0.09375
- wo: bfloat16 [4096, 4096], P('wide', 'narrow'), may hold values from -0.09375 to 0.09375
- wgate: bfloat16 [14336, 4096], P('wide', 'narrow'), may hold values from -0.09375 to 0.09375
- wup: bfloat16 [14336, 4096], P('wide', 'narrow'), may hold values from -0.09375 to 0.09375
- wdown: bfloat16 [14336, 4096], P('wide', 'narrow'), may hold values from -0.125 to 0.125
Outputs:
- hidden_out: bfloat16 [1024, 4096], P('narrow', 'wide')
- new_k_cache: bfloat16 [4, 32768, 128], P('narrow', 'wide')
- new_v_cache: bfloat16 [4, 32768, 128], P('narrow', 'wide')
All inputs are finite; a program needn't handle non-finite values.
Results may differ from a plain program's by a relative error of at most 0.018.
The roundings to bfloat16 on the way count: a program that leaves them out, or rounds other values in their place, can miss the bound.
Values may be sent and summed in bfloat16 or wider, within the bound.
A program may use at most 64 MiB of HBM per device.

v0:
```python
import jax
import jax.numpy as jnp
from jax import lax
from jax.sharding import PartitionSpec as P

QH = 32
KVH = 8
HD = 128
WINDOW = 4096
NEG_FILL = -1e30


def partner(block, axis, stride):
    count = lax.axis_size(axis)
    route = []
    for low in range(count):
        high = low | 1 << stride
        if high != low and high < count:
            route += [(low, high), (high, low)]
    return lax.ppermute(block, axis, route)


def rms_scale(values, weights):
    widened = values.astype(jnp.float32)
    mean_square = jnp.mean(widened * widened, axis=-1, keepdims=True)
    return (widened * lax.rsqrt(mean_square + 1e-05) * weights.astype(jnp.float32)).astype(
        jnp.bfloat16
    )


def times_rows(left, right):
    return lax.dot_general(
        left, right, (((1,), (1,)), ((), ())), preferred_element_type=jnp.float32
    )


def rotate(heads, positions):
    half_width = heads.shape[-1] // 2
    exponent = jnp.arange(half_width, dtype=jnp.float32) * (2.0 / heads.shape[-1])
    frequency = jnp.power(10000.0, -exponent)
    angles = positions.astype(jnp.float32)[:, None] * frequency[None, :]
    cosine = jnp.cos(angles)[:, None, :]
    sine = jnp.sin(angles)[:, None, :]
    widened = heads.astype(jnp.float32)
    first_half = widened[..., :half_width]
    second_half = widened[..., half_width:]
    return jnp.concatenate(
        [first_half * cosine - second_half * sine, second_half * cosine + first_half * sine],
        axis=-1,
    ).astype(jnp.bfloat16)


def gather_cols(block):
    return lax.all_gather(block, "wide", axis=1, tiled=True)


def collect_heads(qkv_piece, sections):
    position = lax.axis_index("wide")
    for bit_index in range(sections):
        other_piece = partner(qkv_piece, "wide", bit_index)
        upper_half = position // 2**bit_index % 2 == 1
        qkv_piece = jnp.where(
            upper_half,
            jnp.concatenate([other_piece, qkv_piece], axis=1),
            jnp.concatenate([qkv_piece, other_piece], axis=1),
        )
    return qkv_piece


def combine(earlier, later):
    highest = jnp.maximum(earlier[0], later[0])
    left_scale = jnp.exp(earlier[0] - highest)
    right_scale = jnp.exp(later[0] - highest)
    return (
        highest,
        earlier[1] * left_scale + later[1] * right_scale,
        earlier[2] * left_scale[..., None] + later[2] * right_scale[..., None],
    )


def empty_state(row_count, group_size):
    return (
        jnp.full((row_count, group_size), NEG_FILL, jnp.float32),
        jnp.zeros((row_count, group_size), jnp.float32),
        jnp.zeros((row_count, group_size, HD), jnp.float32),
    )


def attend(queries, query_pos, keys, values, key_pos, key_live, soft_state):
    row_count, group_size, head_width = queries.shape
    flat_queries = queries.reshape(row_count * group_size, head_width)
    key_count = keys.shape[0]
    block_size = min(512, key_count)
    block_count = key_count // block_size
    lowest = jnp.min(query_pos)
    highest = jnp.max(query_pos)

    def key_step(carry, blocks):
        key_block, value_block, pos_block, live_block = blocks

        def score_block(running):
            peak_old, totals, accum = running
            scores = jnp.einsum(
                "qd,kd->qk", flat_queries, key_block, preferred_element_type=jnp.float32
            )
            scores = scores.reshape(row_count, group_size, block_size) * HD ** (-0.5)
            allowed = (
                live_block[None, :]
                & (pos_block[None, :] <= query_pos[:, None])
                & (pos_block[None, :] > query_pos[:, None] - WINDOW)
            )
            allowed = allowed[:, None, :]
            scores = jnp.where(allowed, scores, NEG_FILL)
            peak_new = jnp.maximum(peak_old, jnp.max(scores, axis=-1))
            factor = jnp.exp(peak_old - peak_new)
            exp_terms = jnp.where(allowed, jnp.exp(scores - peak_new[..., None]), 0.0)
            totals = totals * factor + jnp.sum(exp_terms, axis=-1)
            weights = exp_terms.astype(jnp.bfloat16).reshape(row_count * group_size, block_size)
            mixed = jnp.dot(weights, value_block, preferred_element_type=jnp.float32).reshape(
                row_count, group_size, head_width
            )
            return (peak_new, totals, accum * factor[..., None] + mixed)

        useful = jnp.any(live_block & (pos_block <= highest) & (pos_block > lowest - WINDOW))
        return (lax.cond(useful, score_block, lambda unchanged: unchanged, carry), None)

    blocks = (
        keys.reshape(block_count, block_size, head_width),
        values.reshape(block_count, block_size, head_width),
        key_pos.reshape(block_count, block_size),
        key_live.reshape(block_count, block_size),
    )
    soft_state, _ = lax.scan(key_step, soft_state, blocks)
    return soft_state


def per_device(
    hidden_in, cached_len, k_cache, v_cache, attn_gain, ffn_gain, wqkv, wo, wgate, wup, wdown
):
    qkv_full, out_full, gate_full, up_full, down_full = (
        lax.all_gather(wqkv, "narrow", axis=1, tiled=True),
        lax.all_gather(wo, "narrow", axis=1, tiled=True),
        lax.all_gather(wgate, "narrow", axis=1, tiled=True),
        lax.all_gather(wup, "narrow", axis=1, tiled=True),
        lax.all_gather(wdown, "narrow", axis=1, tiled=True),
    )
    wide_count = lax.axis_size("wide")
    part_count = wide_count // KVH
    sections = part_count.bit_length() - 1
    position = lax.axis_index("wide")
    part_index = position % part_count
    length = cached_len[lax.axis_index("narrow")]
    span_len = hidden_in.shape[0]
    group_size = QH // KVH
    steps_t = jnp.arange(span_len, dtype=jnp.int32)
    query_pos = length + steps_t
    normed_attn = rms_scale(gather_cols(hidden_in), attn_gain)
    qkv_piece = times_rows(normed_attn, qkv_full).astype(jnp.bfloat16)
    grouped = collect_heads(qkv_piece, sections)
    queries = rotate(grouped[:, : group_size * HD].reshape(span_len, group_size, HD), query_pos)
    new_keys = rotate(
        grouped[:, group_size * HD : (group_size + 1) * HD].reshape(span_len, 1, HD), query_pos
    ).reshape(span_len, HD)
    new_vals = grouped[:, (group_size + 1) * HD :]
    cache_keys = k_cache[0]
    cache_vals = v_cache[0]
    block_slots = cache_keys.shape[0]
    slot_pos = part_index * block_slots + jnp.arange(block_slots, dtype=jnp.int32)
    share_rows = span_len // part_count
    start_row = part_index * share_rows
    soft_state = empty_state(span_len, group_size)
    soft_state = attend(
        queries, query_pos, cache_keys, cache_vals, slot_pos, slot_pos < length, soft_state
    )
    soft_state = attend(
        queries,
        query_pos,
        lax.dynamic_slice_in_dim(new_keys, start_row, share_rows, 0),
        lax.dynamic_slice_in_dim(new_vals, start_row, share_rows, 0),
        lax.dynamic_slice_in_dim(query_pos, start_row, share_rows, 0),
        jnp.ones((share_rows,), jnp.bool_),
        soft_state,
    )
    for bit_index in range(sections):
        soft_state = combine(soft_state, partner(soft_state, "wide", bit_index))
    attended = (
        (soft_state[2] / soft_state[1][..., None])
        .astype(jnp.bfloat16)
        .reshape(span_len, group_size * HD)
    )
    width_share = group_size * HD // part_count
    own_cols = lax.dynamic_slice_in_dim(attended, part_index * width_share, width_share, 1)
    mixed_heads = gather_cols(own_cols)
    projected = times_rows(mixed_heads, out_full)
    after_attn = (hidden_in.astype(jnp.float32) + projected).astype(jnp.bfloat16)
    whole_after = gather_cols(after_attn)
    normed_ffn = rms_scale(whole_after, ffn_gain)
    gate_proj = times_rows(normed_ffn, gate_full)
    up_proj = times_rows(normed_ffn, up_full)
    activation = (jax.nn.silu(gate_proj) * up_proj).astype(jnp.bfloat16)
    summed = lax.psum_scatter(
        lax.dot_general(
            down_full, activation, (((0,), (1,)), ((), ())), preferred_element_type=jnp.float32
        ),
        "wide",
        scatter_dimension=0,
        tiled=True,
    )
    hidden_out = (after_attn.astype(jnp.float32) + summed.T).astype(jnp.bfloat16)
    offset = (slot_pos - length) % WINDOW
    fresh_slot = offset < span_len
    pick_row = jnp.minimum(offset, span_len - 1)
    new_k_cache = jnp.where(fresh_slot[:, None], jnp.take(new_keys, pick_row, axis=0), cache_keys)[
        None
    ]
    new_v_cache = jnp.where(fresh_slot[:, None], jnp.take(new_vals, pick_row, axis=0), cache_vals)[
        None
    ]
    return (hidden_out, new_k_cache, new_v_cache)


def solution(mesh):
    return jax.shard_map(
        per_device,
        mesh=mesh,
        in_specs=(
            P("narrow", "wide"),
            P(),
            P("narrow", "wide", None),
            P("narrow", "wide", None),
            P(),
            P(),
            P("wide", "narrow"),
            P("wide", "narrow"),
            P("wide", "narrow"),
            P("wide", "narrow"),
            P("wide", "narrow"),
        ),
        out_specs=(P("narrow", "wide"), P("narrow", "wide", None), P("narrow", "wide", None)),
        check_vma=False,
    )
```

profile of v0, /device:TPU:2, one launch (start us, length us, event | category | flops | bytes accessed | tf_op | source)
XLA Modules:
  0.0 569.9 jit_solution(13301387686112721194)
XLA Ops:
  7.2 0.7 all-gather.7.cloned.1.call-update
  8.0 1.3 dynamic_slice.37
  9.2 1.2 fusion.63
  10.5 1.2 fusion.64
  11.7 0.7 convert_element_type.93
  13.1 2.0 fusion.58
  15.7 14.4 %all_gather.25 = bf16[96,4096]{1,0:T(8,128)(2,1)S(1)} all-gather(bf16[96,1024]{1,0:T(8,128)(2,1)} %param.23), channel_id=1, replica_groups=mesh['wide'=64,'narrow'=4] {'narrow'}, dimensions={1}, use_global_device_ids=true | all-gather | bytes 983040 | tf_op jit(solution)/shard_map/all_gather | solution.py:141
  30.1 61.0 %all-gather.7.cloned.1.call-done = bf16[256,4096]{0,1:T(8,128)(2,1)} async-done(((bf16[256,64]{0,1:T(8,128)(2,1)}), bf16[256,4096]{0,1:T(8,128)(2,1)}) %all-gather.7.cloned.1.call-update) | async-done | bytes 2097168 | tf_op jit(solution)/shard_map/all_gather | solution.py:54
  91.0 2.3 fusion.16
  93.4 0.8 fusion.27
  94.6 1.9 and_reduce_fusion
  97.9 0.7 broadcast_in_dim.114
  99.2 4.4 collective-permute-done.1
  103.6 2.2 collective-permute-start.2
  106.1 5.3 collective-permute-done.2
  113.9 11.8 %conditional.2 = ((f32[256,4]{1,0:T(8,128)S(1)}, f32[256,4]{1,0:T(8,128)}, f32[256,4,128]{2,0,1:T(8,128)S(1)})) conditional(s32[]{:T(128)} %convert_element_type.91, (f32[256,4]{1,0:T(8,128)S(1)}, f32[256,4]{1,0:T(8,128)}, f32[256,4,128]{2,0,1:T(8,128)S(1)}) %tuple.31, (pred[512]{0:T(512)(128)(4,1)S(1)}, s32[512]{0:T(512)S(1)}, s32[256]{0:T(256)S(1)}, ...), branch_computations={%region_5.6_spmd, %region_6.9_spmd} | conditional | flops 273942784 | bytes 13486680 | solution.py:125
  115.1 1.5 fusion
  116.6 0.8 reduce_max.28
  117.4 1.6 max.12
  119.0 1.0 sub.66
  120.0 1.8 fusion.1
  122.0 1.7 multiply_add_fusion
  123.7 1.4 dot_general.9
  125.7 4.8 conditional.3
  125.8 0.7 compare_and_fusion.1
  126.9 0.9 copy.56
  128.6 0.9 multiply_add_fusion.1
  131.2 1.3 collective-permute-done.3
  133.2 1.5 collective-permute-start.10
  135.2 11.6 %collective-permute-done.10 = f32[256,4]{0,1:T(4,128)S(1)} collective-permute-done((f32[256,4]{0,1:T(4,128)S(1)}, f32[256,4]{0,1:T(4,128)S(1)}, u32[]{:S(2)}, u32[]{:S(2)}) %collective-permute-start.10) | collective-permute-done | bytes 4128 | tf_op jit(solution)/shard_map/ppermute | solution.py:20
  147.1 3.5 collective-permute-start.11
  150.7 11.1 %collective-permute-done.11 = f32[256,4]{0,1:T(4,128)S(1)} collective-permute-done((f32[256,4]{0,1:T(4,128)S(1)}, f32[256,4]{0,1:T(4,128)S(1)}, u32[]{:S(2)}, u32[]{:S(2)}) %collective-permute-start.11) | collective-permute-done | bytes 4128 | tf_op jit(solution)/shard_map/ppermute | solution.py:20
  162.7 12.8 %all_gather.27 = bf16[64,4096]{1,0:T(8,128)(2,1)S(1)} all-gather(bf16[64,1024]{1,0:T(8,128)(2,1)S(1)} %copy-done.14), channel_id=1, replica_groups=mesh['wide'=64,'narrow'=4] {'narrow'}, dimensions={1}, use_global_device_ids=true | all-gather | bytes 655360 | tf_op jit(solution)/shard_map/all_gather | solution.py:142
  175.5 61.0 %all-gather.9.cloned.1.call-done = bf16[256,4096]{0,1:T(8,128)(2,1)} async-done(((bf16[256,64]{0,1:T(8,128)(2,1)}), bf16[256,4096]{0,1:T(8,128)(2,1)}) %all-gather.9.cloned.1.call-update) | async-done | bytes 2097168 | tf_op jit(solution)/shard_map/all_gather | solution.py:54
  236.4 2.7 fusion.30
  240.9 73.8 %all-gather.11.cloned.1.call-done = bf16[256,4096]{0,1:T(8,128)(2,1)} async-done(((bf16[256,64]{0,1:T(8,128)(2,1)}), bf16[256,4096]{0,1:T(8,128)(2,1)}) %all-gather.11.cloned.1.call-update) | async-done | bytes 2097168 | tf_op jit(solution)/shard_map/all_gather | solution.py:54
  314.8 2.3 fusion.19
  317.1 27.2 %all-gather.13.cloned.1.call-done = bf16[224,4096]{1,0:T(8,128)(2,1)} async-done(((bf16[224,1024]{1,0:T(8,128)(2,1)}), bf16[224,4096]{1,0:T(8,128)(2,1)}) %all-gather.13.cloned.1.call-update) | async-done | bytes 1835024 | tf_op jit(solution)/shard_map/all_gather | solution.py:143
  344.4 2.3 fusion.31
  346.7 30.5 %all-gather.15.cloned.1.call-done = bf16[224,4096]{1,0:T(8,128)(2,1)} async-done(((bf16[224,1024]{1,0:T(8,128)(2,1)}), bf16[224,4096]{1,0:T(8,128)(2,1)}) %all-gather.15.cloned.1.call-update) | async-done | bytes 1835024 | tf_op jit(solution)/shard_map/all_gather | solution.py:144
  377.3 32.9 %all-gather.17.cloned.1.call-done = bf16[224,4096]{1,0:T(8,128)(2,1)} async-done(((bf16[224,1024]{1,0:T(8,128)(2,1)}), bf16[224,4096]{1,0:T(8,128)(2,1)}) %all-gather.17.cloned.1.call-update) | async-done | bytes 1835024 | tf_op jit(solution)/shard_map/all_gather | solution.py:145
  410.2 6.4 %convolution_bitcast_fusion = f32[4096,256]{1,0:T(8,128)} fusion(bf16[224,4096]{1,0:T(8,128)(2,1)} %all-gather.17.cloned.1.call-done, bf16[224,4096]{1,0:T(8,128)(2,1)} %all-gather.15.cloned.1.call-done, bf16[256,4096]{0,1:T(8,128)(2,1)S(1)} %copy-done, f32[4096]{0:T(1024)S(1)} %convert_element_type.105, f32[256]{0:T(256)S(1)} %add_rsqrt_fusion, ...), kind=kOutput, calls=%fused_computation.32 | convolution fusion | flops 944062464 | bytes 10208256 | tf_op jit(solution)/shard_map/dot_general | solution.py:202
  416.6 0.7 compare_and_fusion.2
  418.2 1.3 gather_fusion
  419.6 1.3 gather_fusion.1
  420.9 0.9 fusion.40
  421.9 139.7 %reduce-scatter.2.cloned.1.call-done = f32[64,256]{1,0:T(8,128)} async-done(((f32[4096,256]{1,0:T(8,128)}), f32[64,256]{1,0:T(8,128)}) %reduce-scatter.2.cloned.1.call-update) | async-done | bytes 65552 | tf_op jit(solution)/shard_map/reduce_scatter | solution.py:201
  561.6 1.5 fusion.52
  (119 shorter events, 14.2 us)
Async XLA Ops:
  7.2 83.9 %all-gather.7.cloned.1.call-start = ((), (), s32[]{:S(2)}) async-start(), calls=%async_computation.1 | async-start | bytes 2129920 | tf_op jit(solution)/shard_map/all_gather | solution.py:54
  7.9 228.5 %all-gather.9.cloned.1.call-start = ((), (), s32[]{:S(2)}) async-start(), calls=%async_computation.2 | async-start | bytes 2129920 | tf_op jit(solution)/shard_map/all_gather | solution.py:54
  91.0 2.3 copy-start.1
  94.2 4.3 collective-permute-start
  98.5 5.0 collective-permute-start.1
  103.6 7.8 %collective-permute-start.2 = (bf16[256,384]{0,1:T(8,128)(2,1)S(1)}, bf16[256,384]{0,1:T(8,128)(2,1)S(1)}, u32[]{:S(2)}, u32[]{:S(2)}) collective-permute-start(bf16[256,384]{0,1:T(8,128)(2,1)S(1)} %maximum_select_fusion.1), channel_id=1, source_target_pairs={{0,16},{16,0},{4,20},{20,4},{8,24},{24,8},{12,28},{28,12},{32,48},... | collective-permute-start | bytes 589832 | tf_op jit(solution)/shard_map/ppermute | solution.py:20
  112.6 1.3 copy-start.9
  112.6 1.3 copy-start.11
  121.8 3.3 copy-start.7
  123.7 2.0 copy-start.2
  125.7 4.1 copy-start.4
  130.5 2.0 collective-permute-start.4
  130.6 1.9 collective-permute-start.3
  131.1 1.4 collective-permute-start.9
  132.5 30.2 %copy-start.14 = (bf16[64,1024]{1,0:T(8,128)(2,1)S(1)}, bf16[64,1024]{1,0:T(8,128)(2,1)}, u32[]{:S(2)}) copy-start(bf16[64,1024]{1,0:T(8,128)(2,1)} %param.24) | copy-start | bytes 393220
  132.6 103.8 %copy-start.13 = (bf16[256,64]{0,1:T(8,128)(2,1)S(1)}, bf16[256,64]{0,1:T(8,128)(2,1)}, u32[]{:S(2)}) copy-start(bf16[256,64]{0,1:T(8,128)(2,1)} %param.17) | copy-start | bytes 98308
  132.6 14.2 %collective-permute-start.6 = (f32[256,4,128]{0,2,1:T(8,128)S(1)}, f32[256,4,128]{0,2,1:T(8,128)S(1)}, u32[]{:S(2)}, u32[]{:S(2)}) collective-permute-start(f32[256,4,128]{0,2,1:T(8,128)S(1)} %multiply_add_fusion.3), channel_id=1, source_target_pairs={{0,8},{8,0},{4,12},{12,4},{16,24},{24,16},{20,28},{28,20},{32,40},... | collective-permute-start | bytes 1572872 | tf_op jit(solution)/shard_map/ppermute | solution.py:20
  133.2 13.6 %collective-permute-start.10 = (f32[256,4]{0,1:T(4,128)S(1)}, f32[256,4]{0,1:T(4,128)S(1)}, u32[]{:S(2)}, u32[]{:S(2)}) collective-permute-start(f32[256,4]{0,1:T(4,128)S(1)} %get-tuple-element.243), channel_id=1, source_target_pairs={{0,8},{8,0},{4,12},{12,4},{16,24},{24,16},{20,28},{28,20},{32,40},... | collective-permute-start | bytes 12296 | tf_op jit(solution)/shard_map/ppermute | solution.py:20
  134.7 12.1 %collective-permute-start.5 = (f32[256,4]{0,1:T(4,128)S(1)}, f32[256,4]{0,1:T(4,128)S(1)}, u32[]{:S(2)}, u32[]{:S(2)}) collective-permute-start(f32[256,4]{0,1:T(4,128)S(1)} %get-tuple-element.246), channel_id=1, source_target_pairs={{0,8},{8,0},{4,12},{12,4},{16,24},{24,16},{20,28},{28,20},{32,40},... | collective-permute-start | bytes 12296 | tf_op jit(solution)/shard_map/ppermute | solution.py:20
  147.0 14.9 %collective-permute-start.8 = (f32[256,4,128]{0,2,1:T(8,128)S(1)}, f32[256,4,128]{0,2,1:T(8,128)S(1)}, u32[]{:S(2)}, u32[]{:S(2)}) collective-permute-start(f32[256,4,128]{0,2,1:T(8,128)S(1)} %multiply_add_fusion.2), channel_id=1, source_target_pairs={{0,16},{16,0},{4,20},{20,4},{8,24},{24,8},{12,28},{28,12},{32,48},... | collective-permute-start | bytes 1572872 | tf_op jit(solution)/shard_map/ppermute | solution.py:20
  147.1 14.8 %collective-permute-start.11 = (f32[256,4]{0,1:T(4,128)S(1)}, f32[256,4]{0,1:T(4,128)S(1)}, u32[]{:S(2)}, u32[]{:S(2)}) collective-permute-start(f32[256,4]{0,1:T(4,128)S(1)} %get-tuple-element.239), channel_id=1, source_target_pairs={{0,16},{16,0},{4,20},{20,4},{8,24},{24,8},{12,28},{28,12},{32,48},... | collective-permute-start | bytes 12296 | tf_op jit(solution)/shard_map/ppermute | solution.py:20
  150.6 11.3 %collective-permute-start.7 = (f32[256,4]{0,1:T(4,128)S(1)}, f32[256,4]{0,1:T(4,128)S(1)}, u32[]{:S(2)}, u32[]{:S(2)}) collective-permute-start(f32[256,4]{0,1:T(4,128)S(1)} %get-tuple-element.242), channel_id=1, source_target_pairs={{0,16},{16,0},{4,20},{20,4},{8,24},{24,8},{12,28},{28,12},{32,48},... | collective-permute-start | bytes 12296 | tf_op jit(solution)/shard_map/ppermute | solution.py:20
  162.6 152.1 %all-gather.11.cloned.1.call-start = ((), (), s32[]{:S(2)}) async-start(), calls=%async_computation.3 | async-start | bytes 2129920 | tf_op jit(solution)/shard_map/all_gather | solution.py:54
  175.5 65.5 %copy-start.15 = (bf16[4096]{0:T(1024)(128)(2,1)S(1)}, bf16[4096]{0:T(1024)(128)(2,1)}, u32[]{:S(2)}) copy-start(bf16[4096]{0:T(1024)(128)(2,1)} %param.22) | copy-start | bytes 24580
  239.1 105.2 %all-gather.13.cloned.1.call-start = ((), (), s32[]{:S(2)}) async-start(), calls=%async_computation.4 | async-start | bytes 2293760 | tf_op jit(solution)/shard_map/all_gather | solution.py:143
  239.7 137.5 %all-gather.15.cloned.1.call-start = ((), (), s32[]{:S(2)}) async-start(), calls=%async_computation.5 | async-start | bytes 2293760 | tf_op jit(solution)/shard_map/all_gather | solution.py:144
  240.3 169.9 %all-gather.17.cloned.1.call-start = ((), (), s32[]{:S(2)}) async-start(), calls=%async_computation.6 | async-start | bytes 2293760 | tf_op jit(solution)/shard_map/all_gather | solution.py:145
  240.9 320.7 %reduce-scatter.2.cloned.1.call-start = ((), (), s32[]{:S(2)}) async-start(), calls=%async_computation.7 | async-start | bytes 4259840 | tf_op jit(solution)/shard_map/reduce_scatter | solution.py:201
  314.8 29.6 %copy-start = (bf16[256,4096]{0,1:T(8,128)(2,1)S(1)}, bf16[256,4096]{0,1:T(8,128)(2,1)}, u32[]{:S(2)}) copy-start(bf16[256,4096]{0,1:T(8,128)(2,1)} %all-gather.11.cloned.1.call-done) | copy-start | bytes 6291460
  416.5 1.4 copy-start.3
  416.5 1.6 copy-start.10
  416.5 1.6 copy-start.12
  416.6 4.4 copy-start.5
  416.6 4.4 copy-start.6
  416.6 145.0 %copy-start.8 = (bf16[256,64]{0,1:T(8,128)(2,1)S(1)}, bf16[256,64]{0,1:T(8,128)(2,1)}, u32[]{:S(2)}) copy-start(bf16[256,64]{0,1:T(8,128)(2,1)} %fusion.30) | copy-start | bytes 98308
Sparse Core Ops, SparseCore 0:
  10.8 80.2 all-gather.6
  162.8 73.6 all-gather.8
  239.8 74.9 all-gather.10
  316.4 27.8 all-gather.12
  346.0 31.1 all-gather.14
  378.9 31.1 all-gather.16
  416.7 144.8 reduce-scatter.1
where the time goes:
time: 570 us
  waiting for transfers between devices  462 us (81%)
  blocking collectives  27.1 us (5%)
  other arithmetic  25.7 us (5%)
  between operations  16.5 us (3%)
  matrix products  14.7 us (3%)
  local copies, waits for them, and re-layouts  12.8 us (2%)
  starting transfers between devices  10.4 us (2%)
    all_gather x3, waiting for transfers between devices, gather_cols(): return lax.all_gather(block, 'wide', axis=1, tiled=True)  196 us
    reduce_scatter x1, waiting for transfers between devices, per_device(): lax.psum_scatter(lax.dot_general(down_full, activation, (((0,), (1,)), ((...  140 us
    ppermute x12, waiting for transfers between devices, partner(): return lax.ppermute(block, axis, route)  33.9 us
    all_gather x1, waiting for transfers between devices, per_device(): lax.all_gather(wdown, 'narrow', axis=1, tiled=True)  32.9 us
    all_gather x1, waiting for transfers between devices, per_device(): lax.all_gather(wup, 'narrow', axis=1, tiled=True)  30.5 us
    all_gather x1, waiting for transfers between devices, per_device(): lax.all_gather(wgate, 'narrow', axis=1, tiled=True)  27.2 us
    all_gather x1, blocking collectives, per_device(): lax.all_gather(wqkv, 'narrow', axis=1, tiled=True)  14.4 us
    all_gather x1, blocking collectives, per_device(): lax.all_gather(wo, 'narrow', axis=1, tiled=True)  12.8 us
  transfers between devices with their start and end apart: 19, of which 12 were waited for; matrix products, arithmetic and copies ran while one was open for 3% of the time, Pallas kernels for 0%

commit v1 on v0

--- a/solution.py
+++ b/solution.py
@@ -8,6 +8,37 @@
 HD = 128
 WINDOW = 4096
 NEG_FILL = -1e30
+
+
+def apply_tiles(z, axis_id):
+    moved, piece_next, everything = (
+        jax.lax.axis_size(axis_id),
+        jax.lax.axis_index(axis_id),
+        z.shape[1],
+    )
+    inbox = []
+    for i, dd in enumerate(z.shape):
+        inbox.append(dd * moved if i == 1 else dd)
+    part_next = jnp.zeros(inbox, z.dtype)
+    outcome_arr = lax.dynamic_update_slice_in_dim(part_next, z, piece_next * everything, axis=1)
+    m_next = step_out = z
+    for ix in [*range(1, moved // 2 + 1)]:
+        runs = []
+        for i in [*range(moved)]:
+            runs.append((i, (i + 1) % moved))
+        m_next = jax.lax.ppermute(m_next, axis_name=axis_id, perm=runs)
+        outcome_arr = lax.dynamic_update_slice_in_dim(
+            outcome_arr, m_next, (piece_next - ix) % moved * everything, axis=1
+        )
+        if 2 * ix < moved:
+            by_rank = []
+            for i in tuple(range(moved)):
+                by_rank.append((i, (i - 1) % moved))
+            step_out = jax.lax.ppermute(step_out, axis_name=axis_id, perm=by_rank)
+            outcome_arr = lax.dynamic_update_slice_in_dim(
+                outcome_arr, step_out, (piece_next + ix) % moved * everything, axis=1
+            )
+    return outcome_arr
 
 
 def partner(block, axis, stride):
@@ -140,7 +171,7 @@
     qkv_full, out_full, gate_full, up_full, down_full = (
         lax.all_gather(wqkv, "narrow", axis=1, tiled=True),
         lax.all_gather(wo, "narrow", axis=1, tiled=True),
-        lax.all_gather(wgate, "narrow", axis=1, tiled=True),
+        apply_tiles(wgate, "narrow"),
         lax.all_gather(wup, "narrow", axis=1, tiled=True),
         lax.all_gather(wdown, "narrow", axis=1, tiled=True),
     )

time: 570 us -> 538 us (0.944)
  waiting for transfers between devices: 462 us -> 421 us
    all_gather x1 -> x0, waiting for transfers between devices: 27.2 us -> none  [per_device(): lax.all_gather(wgate, 'narrow', axis=1, tiled=True)]
    all_gather x3, waiting for transfers between devices: 196 us -> 171 us  [gather_cols(): return lax.all_gather(block, 'wide', axis=1, tiled=True)]
    ppermute x0 -> x3, waiting for transfers between devices: none -> 17.1 us  [the longest x2 17 us: apply_tiles(): m_next = jax.lax.ppermute(m_next, axis_name=axis_id, perm=runs)]
  transfers between devices with their start and end apart: 19 -> 21, of which waited for: 12 -> 13; matrix products, arithmetic and copies ran while one was open for 3% -> 5% of each run, Pallas kernels for 0% -> 0%
where the time goes in v1:
time: 538 us; the launch traced here: 537 us
  waiting for transfers between devices  421 us (78%)
  blocking collectives  27.3 us (5%)
  other arithmetic  25.3 us (5%)
  local copies, waits for them, and re-layouts  17.7 us (3%)
  between operations  16.4 us (3%)
  matrix products  14.7 us (3%)
  starting transfers between devices  13.9 us (3%)
    all_gather x3, waiting for transfers between devices, gather_cols(): return lax.all_gather(block, 'wide', axis=1, tiled=True)  171 us
    reduce_scatter x1, waiting for transfers between devices, per_device(): lax.psum_scatter(lax.dot_general(down_full, activation, (((0,), (1,)), ((...  140 us
    ppermute x12, waiting for transfers between devices, partner(): return lax.ppermute(block, axis, route)  33.9 us
    all_gather x1, waiting for transfers between devices, per_device(): lax.all_gather(wdown, 'narrow', axis=1, tiled=True)  30.5 us
    all_gather x1, waiting for transfers between devices, per_device(): lax.all_gather(wup, 'narrow', axis=1, tiled=True)  27.2 us
    ppermute x2, waiting for transfers between devices, apply_tiles(): m_next = jax.lax.ppermute(m_next, axis_name=axis_id, perm=runs)  17 us
    all_gather x1, blocking collectives, per_device(): lax.all_gather(wqkv, 'narrow', axis=1, tiled=True)  14.4 us
    all_gather x1, blocking collectives, per_device(): lax.all_gather(wo, 'narrow', axis=1, tiled=True)  12.9 us
  transfers between devices with their start and end apart: 21, of which 13 were waited for; matrix products, arithmetic and copies ran while one was open for 5% of the time, Pallas kernels for 0%

profile of v1, /device:TPU:2, one launch (start us, length us, event | category | flops | bytes accessed | tf_op | source)
XLA Modules:
  0.0 536.9 jit_solution(6991245326974893274)
XLA Ops:
  8.0 1.2 dynamic_slice.37
  9.2 1.2 fusion.61
  10.4 1.2 fusion.62
  12.9 1.9 fusion.56
  15.4 14.4 %all_gather.22 = bf16[96,4096]{1,0:T(8,128)(2,1)S(1)} all-gather(bf16[96,1024]{1,0:T(8,128)(2,1)} %param.23), channel_id=1, replica_groups=mesh['wide'=64,'narrow'=4] {'narrow'}, dimensions={1}, use_global_device_ids=true | all-gather | bytes 983040 | tf_op jit(solution)/shard_map/all_gather | solution.py:172
  29.7 61.3 %all-gather.6.cloned.1.call-done = bf16[256,4096]{0,1:T(8,128)(2,1)} async-done(((bf16[256,64]{0,1:T(8,128)(2,1)}), bf16[256,4096]{0,1:T(8,128)(2,1)}) %all-gather.6.cloned.1.call-update) | async-done | bytes 2097168 | tf_op jit(solution)/shard_map/all_gather | solution.py:85
  91.0 2.3 fusion.16
  94.6 1.9 and_reduce_fusion
  99.1 4.4 collective-permute-done.1
  103.5 2.2 collective-permute-start.2
  106.0 5.3 collective-permute-done.2
  113.8 11.8 %conditional.2 = ((f32[256,4]{1,0:T(8,128)S(1)}, f32[256,4]{1,0:T(8,128)}, f32[256,4,128]{2,0,1:T(8,128)S(1)})) conditional(s32[]{:T(128)} %convert_element_type.91, (f32[256,4]{1,0:T(8,128)S(1)}, f32[256,4]{1,0:T(8,128)}, f32[256,4,128]{2,0,1:T(8,128)S(1)}) %tuple.31, (pred[512]{0:T(512)(128)(4,1)S(1)}, s32[512]{0:T(512)S(1)}, s32[256]{0:T(256)S(1)}, ...), branch_computations={%region_5.6_spmd, %region_6.9_spmd} | conditional | flops 273942784 | bytes 13486680 | solution.py:156
  115.1 1.5 fusion
  117.3 1.6 max.12
  118.9 1.0 sub.70
  119.9 1.8 fusion.1
  121.9 1.7 multiply_add_fusion
  123.6 1.4 dot_general.9
  125.6 4.8 conditional.3
  126.9 0.9 copy.56
  128.5 0.9 multiply_add_fusion.1
  131.1 1.3 collective-permute-done.3
  133.1 1.5 collective-permute-start.10
  135.2 11.6 %collective-permute-done.10 = f32[256,4]{0,1:T(4,128)S(1)} collective-permute-done((f32[256,4]{0,1:T(4,128)S(1)}, f32[256,4]{0,1:T(4,128)S(1)}, u32[]{:S(2)}, u32[]{:S(2)}) %collective-permute-start.10) | collective-permute-done | bytes 4128 | tf_op jit(solution)/shard_map/ppermute | solution.py:51
  147.0 3.5 collective-permute-start.11
  150.6 11.1 %collective-permute-done.11 = f32[256,4]{0,1:T(4,128)S(1)} collective-permute-done((f32[256,4]{0,1:T(4,128)S(1)}, f32[256,4]{0,1:T(4,128)S(1)}, u32[]{:S(2)}, u32[]{:S(2)}) %collective-permute-start.11) | collective-permute-done | bytes 4128 | tf_op jit(solution)/shard_map/ppermute | solution.py:51
  162.6 12.9 %all_gather.24 = bf16[64,4096]{1,0:T(8,128)(2,1)S(1)} all-gather(bf16[64,1024]{1,0:T(8,128)(2,1)S(1)} %copy-done.15), channel_id=1, replica_groups=mesh['wide'=64,'narrow'=4] {'narrow'}, dimensions={1}, use_global_device_ids=true | all-gather | bytes 655360 | tf_op jit(solution)/shard_map/all_gather | solution.py:173
  175.5 60.8 %all-gather.8.cloned.1.call-done = bf16[256,4096]{0,1:T(8,128)(2,1)} async-done(((bf16[256,64]{0,1:T(8,128)(2,1)}), bf16[256,4096]{0,1:T(8,128)(2,1)}) %all-gather.8.cloned.1.call-update) | async-done | bytes 2097168 | tf_op jit(solution)/shard_map/all_gather | solution.py:85
  236.4 2.7 fusion.29
  240.3 1.5 collective-permute-start.12
  242.4 10.7 %collective-permute-done.12 = bf16[224,1024]{1,0:T(8,128)(2,1)S(1)} collective-permute-done((bf16[224,1024]{1,0:T(8,128)(2,1)S(1)}, bf16[224,1024]{1,0:T(8,128)(2,1)S(1)}, u32[]{:S(2)}, u32[]{:S(2)}) %collective-permute-start.12) | collective-permute-done | bytes 458784 | tf_op jit(solution)/shard_map/ppermute | solution.py:29
  253.1 1.5 collective-permute-start.14
  254.5 1.5 broadcast_in_dim.119
  256.0 0.9 constant_dynamic-update-slice_fusion.3
  257.7 0.8 constant_dynamic-update-slice_fusion.1
  258.6 6.4 %collective-permute-done.14 = bf16[224,1024]{1,0:T(8,128)(2,1)S(1)} collective-permute-done((bf16[224,1024]{1,0:T(8,128)(2,1)S(1)}, bf16[224,1024]{1,0:T(8,128)(2,1)S(1)}, u32[]{:S(2)}, u32[]{:S(2)}) %collective-permute-start.14) | collective-permute-done | bytes 458784 | tf_op jit(solution)/shard_map/ppermute | solution.py:29
  265.0 0.9 constant_dynamic-update-slice_fusion
  265.8 48.9 %all-gather.10.cloned.1.call-done = bf16[256,4096]{0,1:T(8,128)(2,1)} async-done(((bf16[256,64]{0,1:T(8,128)(2,1)}), bf16[256,4096]{0,1:T(8,128)(2,1)}) %all-gather.10.cloned.1.call-update) | async-done | bytes 2097168 | tf_op jit(solution)/shard_map/all_gather | solution.py:85
  314.7 2.3 fusion.19
  317.0 27.2 %all-gather.12.cloned.1.call-done = bf16[224,4096]{1,0:T(8,128)(2,1)} async-done(((bf16[224,1024]{1,0:T(8,128)(2,1)}), bf16[224,4096]{1,0:T(8,128)(2,1)}) %all-gather.12.cloned.1.call-update) | async-done | bytes 1835024 | tf_op jit(solution)/shard_map/all_gather | solution.py:175
  344.3 2.4 fusion.32
  346.6 30.5 %all-gather.14.cloned.1.call-done = bf16[224,4096]{1,0:T(8,128)(2,1)} async-done(((bf16[224,1024]{1,0:T(8,128)(2,1)}), bf16[224,4096]{1,0:T(8,128)(2,1)}) %all-gather.14.cloned.1.call-update) | async-done | bytes 1835024 | tf_op jit(solution)/shard_map/all_gather | solution.py:176
  377.2 6.4 %convolution_bitcast_fusion = f32[4096,256]{1,0:T(8,128)} fusion(bf16[224,4096]{1,0:T(8,128)(2,1)} %all-gather.14.cloned.1.call-done, f32[256,224]{0,1:T(8,128)S(1)} %fusion.32, bf16[224,4096]{1,0:T(8,128)(2,1)} %constant_dynamic-update-slice_fusion, bf16[256,4096]{0,1:T(8,128)(2,1)S(1)} %copy-done, f32[4096]{0:T(1024)S(1)} %convert_element_type.105, ...), kind=kOutput, calls=%fused_computation.32 | convolution fusion | flops 944062464 | bytes 10208256 | tf_op jit(solution)/shard_map/dot_general | solution.py:233
  385.2 1.3 gather_fusion
  386.5 1.3 gather_fusion.1
  387.9 0.9 fusion.38
  388.8 139.9 %reduce-scatter.2.cloned.1.call-done = f32[64,256]{1,0:T(8,128)} async-done(((f32[4096,256]{1,0:T(8,128)}), f32[64,256]{1,0:T(8,128)}) %reduce-scatter.2.cloned.1.call-update) | async-done | bytes 65552 | tf_op jit(solution)/shard_map/reduce_scatter | solution.py:232
  528.6 1.5 fusion.50
  (129 shorter events, 20.0 us)
Async XLA Ops:
  7.2 83.9 %all-gather.6.cloned.1.call-start = ((), (), s32[]{:S(2)}) async-start(), calls=%async_computation.1 | async-start | bytes 2129920 | tf_op jit(solution)/shard_map/all_gather | solution.py:85
  7.9 228.5 %all-gather.8.cloned.1.call-start = ((), (), s32[]{:S(2)}) async-start(), calls=%async_computation.2 | async-start | bytes 2129920 | tf_op jit(solution)/shard_map/all_gather | solution.py:85
  91.0 2.3 copy-start.1
  94.2 4.2 collective-permute-start
  98.4 5.0 collective-permute-start.1
  103.5 7.8 %collective-permute-start.2 = (bf16[256,384]{0,1:T(8,128)(2,1)S(1)}, bf16[256,384]{0,1:T(8,128)(2,1)S(1)}, u32[]{:S(2)}, u32[]{:S(2)}) collective-permute-start(bf16[256,384]{0,1:T(8,128)(2,1)S(1)} %maximum_select_fusion.1), channel_id=1, source_target_pairs={{0,16},{16,0},{4,20},{20,4},{8,24},{24,8},{12,28},{28,12},{32,48},... | collective-permute-start | bytes 589832 | tf_op jit(solution)/shard_map/ppermute | solution.py:51
  112.5 1.3 copy-start.10
  112.5 1.3 copy-start.12
  121.7 3.3 copy-start.7
  123.6 2.0 copy-start.2
  125.6 4.1 copy-start.4
  130.4 2.0 collective-permute-start.4
  130.5 1.9 collective-permute-start.3
  131.0 1.4 collective-permute-start.9
  132.4 30.2 %copy-start.15 = (bf16[64,1024]{1,0:T(8,128)(2,1)S(1)}, bf16[64,1024]{1,0:T(8,128)(2,1)}, u32[]{:S(2)}) copy-start(bf16[64,1024]{1,0:T(8,128)(2,1)} %param.24) | copy-start | bytes 393220
  132.5 103.8 %copy-start.14 = (bf16[256,64]{0,1:T(8,128)(2,1)S(1)}, bf16[256,64]{0,1:T(8,128)(2,1)}, u32[]{:S(2)}) copy-start(bf16[256,64]{0,1:T(8,128)(2,1)} %param.17) | copy-start | bytes 98308
  132.6 14.2 %collective-permute-start.6 = (f32[256,4,128]{0,2,1:T(8,128)S(1)}, f32[256,4,128]{0,2,1:T(8,128)S(1)}, u32[]{:S(2)}, u32[]{:S(2)}) collective-permute-start(f32[256,4,128]{0,2,1:T(8,128)S(1)} %multiply_add_fusion.3), channel_id=1, source_target_pairs={{0,8},{8,0},{4,12},{12,4},{16,24},{24,16},{20,28},{28,20},{32,40},... | collective-permute-start | bytes 1572872 | tf_op jit(solution)/shard_map/ppermute | solution.py:51
  133.1 13.6 %collective-permute-start.10 = (f32[256,4]{0,1:T(4,128)S(1)}, f32[256,4]{0,1:T(4,128)S(1)}, u32[]{:S(2)}, u32[]{:S(2)}) collective-permute-start(f32[256,4]{0,1:T(4,128)S(1)} %get-tuple-element.243), channel_id=1, source_target_pairs={{0,8},{8,0},{4,12},{12,4},{16,24},{24,16},{20,28},{28,20},{32,40},... | collective-permute-start | bytes 12296 | tf_op jit(solution)/shard_map/ppermute | solution.py:51
  134.7 12.1 %collective-permute-start.5 = (f32[256,4]{0,1:T(4,128)S(1)}, f32[256,4]{0,1:T(4,128)S(1)}, u32[]{:S(2)}, u32[]{:S(2)}) collective-permute-start(f32[256,4]{0,1:T(4,128)S(1)} %get-tuple-element.246), channel_id=1, source_target_pairs={{0,8},{8,0},{4,12},{12,4},{16,24},{24,16},{20,28},{28,20},{32,40},... | collective-permute-start | bytes 12296 | tf_op jit(solution)/shard_map/ppermute | solution.py:51
  146.9 14.9 %collective-permute-start.8 = (f32[256,4,128]{0,2,1:T(8,128)S(1)}, f32[256,4,128]{0,2,1:T(8,128)S(1)}, u32[]{:S(2)}, u32[]{:S(2)}) collective-permute-start(f32[256,4,128]{0,2,1:T(8,128)S(1)} %multiply_add_fusion.2), channel_id=1, source_target_pairs={{0,16},{16,0},{4,20},{20,4},{8,24},{24,8},{12,28},{28,12},{32,48},... | collective-permute-start | bytes 1572872 | tf_op jit(solution)/shard_map/ppermute | solution.py:51
  147.0 14.8 %collective-permute-start.11 = (f32[256,4]{0,1:T(4,128)S(1)}, f32[256,4]{0,1:T(4,128)S(1)}, u32[]{:S(2)}, u32[]{:S(2)}) collective-permute-start(f32[256,4]{0,1:T(4,128)S(1)} %get-tuple-element.239), channel_id=1, source_target_pairs={{0,16},{16,0},{4,20},{20,4},{8,24},{24,8},{12,28},{28,12},{32,48},... | collective-permute-start | bytes 12296 | tf_op jit(solution)/shard_map/ppermute | solution.py:51
  150.5 11.3 %collective-permute-start.7 = (f32[256,4]{0,1:T(4,128)S(1)}, f32[256,4]{0,1:T(4,128)S(1)}, u32[]{:S(2)}, u32[]{:S(2)}) collective-permute-start(f32[256,4]{0,1:T(4,128)S(1)} %get-tuple-element.242), channel_id=1, source_target_pairs={{0,16},{16,0},{4,20},{20,4},{8,24},{24,8},{12,28},{28,12},{32,48},... | collective-permute-start | bytes 12296 | tf_op jit(solution)/shard_map/ppermute | solution.py:51
  162.6 77.7 %copy-start.8 = (bf16[224,1024]{1,0:T(8,128)(2,1)S(1)}, bf16[224,1024]{1,0:T(8,128)(2,1)}, u32[]{:S(2)}) copy-start(bf16[224,1024]{1,0:T(8,128)(2,1)} %param.25) | copy-start | bytes 1376260
  162.6 92.0 %copy-start.16 = (bf16[4096]{0:T(1024)(128)(2,1)S(1)}, bf16[4096]{0:T(1024)(128)(2,1)}, u32[]{:S(2)}) copy-start(bf16[4096]{0:T(1024)(128)(2,1)} %param.22) | copy-start | bytes 24580
  162.6 152.1 %all-gather.10.cloned.1.call-start = ((), (), s32[]{:S(2)}) async-start(), calls=%async_computation.3 | async-start | bytes 2129920 | tf_op jit(solution)/shard_map/all_gather | solution.py:85
  239.1 105.2 %all-gather.12.cloned.1.call-start = ((), (), s32[]{:S(2)}) async-start(), calls=%async_computation.4 | async-start | bytes 2293760 | tf_op jit(solution)/shard_map/all_gather | solution.py:175
  239.6 137.5 %all-gather.14.cloned.1.call-start = ((), (), s32[]{:S(2)}) async-start(), calls=%async_computation.5 | async-start | bytes 2293760 | tf_op jit(solution)/shard_map/all_gather | solution.py:176
  240.2 288.4 %reduce-scatter.2.cloned.1.call-start = ((), (), s32[]{:S(2)}) async-start(), calls=%async_computation.6 | async-start | bytes 4259840 | tf_op jit(solution)/shard_map/reduce_scatter | solution.py:232
  240.3 12.8 %collective-permute-start.12 = (bf16[224,1024]{1,0:T(8,128)(2,1)S(1)}, bf16[224,1024]{1,0:T(8,128)(2,1)S(1)}, u32[]{:S(2)}, u32[]{:S(2)}) collective-permute-start(bf16[224,1024]{1,0:T(8,128)(2,1)S(1)} %copy-done.8), channel_id=1, source_target_pairs={{0,1},{1,2},{2,3},{3,0},{4,5},{5,6},{6,7},{7,4},{8,9},{9,10},{10,1... | collective-permute-start | bytes 1376264 | tf_op jit(solution)/shard_map/ppermute | solution.py:29
  241.8 15.9 %collective-permute-start.13 = (bf16[224,1024]{1,0:T(8,128)(2,1)S(1)}, bf16[224,1024]{1,0:T(8,128)(2,1)S(1)}, u32[]{:S(2)}, u32[]{:S(2)}) collective-permute-start(bf16[224,1024]{1,0:T(8,128)(2,1)S(1)} %copy-done.8), channel_id=1, source_target_pairs={{0,3},{1,0},{2,1},{3,2},{4,7},{5,4},{6,5},{7,6},{8,11},{9,8},{10,9... | collective-permute-start | bytes 1376264 | tf_op jit(solution)/shard_map/ppermute | solution.py:37
  253.1 11.9 %collective-permute-start.14 = (bf16[224,1024]{1,0:T(8,128)(2,1)S(1)}, bf16[224,1024]{1,0:T(8,128)(2,1)S(1)}, u32[]{:S(2)}, u32[]{:S(2)}) collective-permute-start(bf16[224,1024]{1,0:T(8,128)(2,1)S(1)} %collective-permute-done.12), channel_id=1, source_target_pairs={{0,1},{1,2},{2,3},{3,0},{4,5},{5,6},{6,7},{7,4},{8,9},{9,10},{10,1... | collective-permute-start | bytes 1376264 | tf_op jit(solution)/shard_map/ppermute | solution.py:29
  314.7 29.6 %copy-start = (bf16[256,4096]{0,1:T(8,128)(2,1)S(1)}, bf16[256,4096]{0,1:T(8,128)(2,1)}, u32[]{:S(2)}) copy-start(bf16[256,4096]{0,1:T(8,128)(2,1)} %all-gather.10.cloned.1.call-done) | copy-start | bytes 6291460
  383.6 1.3 copy-start.3
  383.6 1.4 copy-start.11
  383.6 1.5 copy-start.13
  383.6 4.3 copy-start.5
  383.6 4.3 copy-start.6
  383.6 145.0 %copy-start.9 = (bf16[256,64]{0,1:T(8,128)(2,1)S(1)}, bf16[256,64]{0,1:T(8,128)(2,1)}, u32[]{:S(2)}) copy-start(bf16[256,64]{0,1:T(8,128)(2,1)} %fusion.29) | copy-start | bytes 98308
Sparse Core Ops, SparseCore 0:
  10.8 80.2 all-gather.5
  162.7 73.6 all-gather.7
  239.7 74.9 all-gather.9
  316.4 27.8 all-gather.11
  345.9 31.1 all-gather.13
  383.7 144.8 reduce-scatter.1
